TPU v7x, 512 devices: a whole 4x8x8 slice. The times are simulated.
512 devices in a mesh: ctx: 32 (over y, z_hi, core), ch: 16 (over z_lo, x).
Axes of the slice: x: 4, y: 8, z: 8 (z_hi: 2, z_lo: 4; z = z_hi * 4 + z_lo), core: 2. Of those that a mesh axis runs over, the one named last changes fastest.
Arguments:
- query_proj: bfloat16 [16384, 4096], P('ctx', 'ch'), may hold values from -6 to 6
- key_proj: bfloat16 [16384, 4096], P('ctx', 'ch'), may hold values from -6 to 6
- value_proj: bfloat16 [16384, 4096], P('ctx', 'ch'), may hold values from -6 to 6
- out_grad: bfloat16 [16384, 4096], P('ctx', 'ch'), may hold values from -6 to 6
- long_filter: bfloat16 [4096, 16384], P(None, ('ch', 'ctx')), as said below
- skip_gain: float32 [4096], P('ch'), may hold values from -4 to 4
Outputs:
- output: bfloat16 [16384, 4096], P('ctx', 'ch')
- query_grad: bfloat16 [16384, 4096], P('ctx', 'ch')
- key_grad: bfloat16 [16384, 4096], P('ctx', 'ch')
- value_grad: bfloat16 [16384, 4096], P('ctx', 'ch')
Inputs may be any that keep to these rules, and one draw needn't show every extreme that they name: `long_filter`: each channel's filter is a rough sequence of taps under an envelope that falls with the tap index.
All inputs are finite; a program needn't handle non-finite values.
Results may differ from a plain program's by a relative error of at most 0.007.
Values may be sent and summed in bfloat16 or wider, within the bound.
A program may use at most 64 MiB of HBM per device.

v0:
```python
import jax
import jax.numpy as jnp
from jax import lax
from jax.experimental import pallas as pl
from jax.experimental.pallas import tpu as pltpu
from jax.sharding import PartitionSpec as P

CTX = 32
CH = 16
MINE = 8
ROWS = 64
BLK = 256
TAPS = 128
TBLK = 128
SEGS = 4
PER = 16
MESH = pl.DeviceIdType.MESH
F32 = jnp.float32
BF16 = jnp.bfloat16


def eye(size, flip=False):
    row = lax.broadcasted_iota(jnp.int32, (size, size), 0)
    col = lax.broadcasted_iota(jnp.int32, (size, size), 1)
    if flip:
        col = size - 1 - col
    return (row == col).astype(F32).astype(BF16)


def times_transposed(left, right):
    return lax.dot_general(left, right, (((1,), (1,)), ((), ())), preferred_element_type=F32)


def gate(left, right):
    return (left.astype(F32) * right.astype(F32)).astype(BF16)


def ctx_copy(src, dst, send_sem, recv_sem, peer):
    return pltpu.make_async_remote_copy(
        src_ref=src, dst_ref=dst, send_sem=send_sem, recv_sem=recv_sem,
        device_id={"ctx": peer}, device_id_type=MESH,
    )


def ch_copy(src, dst, send_sem, recv_sem, peer):
    return pltpu.make_async_remote_copy(
        src_ref=src, dst_ref=dst, send_sem=send_sem, recv_sem=recv_sem,
        device_id={"ch": peer}, device_id_type=MESH,
    )


def convolve_kernel(
    query, key, value, grad, taps, back,
    taps_rows, taps_send, taps_mid, taps_send2, taps_recv2, taps_wide,
    send, recv, rows_in, rows_out, back_send, blocks, shifted, lhs, acc,
    local_sem, fs1, fr1, fs2, fr2, ss, sr, bs, br,
):
    me = lax.axis_index("ctx")
    my_ch = lax.axis_index("ch")
    barrier = pltpu.get_barrier_semaphore()

    def ctx_peer(k):
        return lax.rem(me + k, CTX)

    def ch_peer(k):
        return lax.rem(my_ch + k, CH)

    @pl.loop(1, CTX)
    def _(k):
        pl.semaphore_signal(barrier, inc=1, device_id={"ctx": ctx_peer(k)}, device_id_type=MESH)

    @pl.loop(1, CH)
    def _(k):
        pl.semaphore_signal(barrier, inc=1, device_id={"ch": ch_peer(k)}, device_id_type=MESH)

    taps_rows[...] = taps[...].astype(F32).reshape(CH * CTX, MINE, 32)
    small = eye(32)

    @pl.loop(0, CTX)
    def _(p):
        tile = taps_rows[pl.ds(p, CH, stride=CTX)].reshape(CH * MINE, 32).astype(BF16)
        taps_send[p] = times_transposed(small, tile).astype(BF16)

    pl.semaphore_wait(barrier, CTX - 1 + CH - 1)

    @pl.loop(1, CTX)
    def _(k):
        p = ctx_peer(k)
        ctx_copy(taps_send.at[p], taps_mid.at[me], fs1.at[p], fr1.at[me], p).start()

    own1 = pltpu.make_async_copy(taps_send.at[me], taps_mid.at[me], local_sem.at[0])
    own1.start()

    unit = eye(BLK)
    mirror = eye(BLK, True)
    for half in range(2):
        toks = pl.ds(BLK * half, BLK)
        gated = times_transposed(unit, gate(key[toks, :], value[toks, :]))
        turned = jnp.dot(mirror, gate(grad[toks, :], query[toks, :]), preferred_element_type=F32)
        graded = times_transposed(unit, turned.astype(BF16))
        both = jnp.concatenate(
            [gated.reshape(CTX, MINE, BLK), graded.reshape(CTX, MINE, BLK)], axis=1
        )
        send[:, half] = both.astype(BF16)

    @pl.loop(1, CTX)
    def _(k):
        p = ctx_peer(k)
        ctx_copy(send.at[p], recv.at[me], ss.at[p], sr.at[me], p).start()

    own2 = pltpu.make_async_copy(send.at[me], recv.at[me], local_sem.at[1])
    own2.start()

    own1.wait()

    @pl.loop(1, CTX)
    def _(k):
        p = ctx_peer(k)
        ctx_copy(taps_send.at[p], taps_mid.at[p], fs1.at[p], fr1.at[p], p).wait_recv()

    unit_t = eye(TAPS)
    for b in range(8):
        tile = taps_mid[pl.ds(4 * b, 4)].reshape(TAPS, CH * MINE)
        turned = times_transposed(unit_t, tile)
        taps_send2[:, :, pl.ds(TAPS * b, TAPS)] = turned.reshape(CH, MINE, TAPS).astype(BF16)

    @pl.loop(1, CH)
    def _(k):
        p = ch_peer(k)
        ch_copy(taps_send2.at[p], taps_recv2.at[my_ch], fs2.at[p], fr2.at[my_ch], p).start()

    own3 = pltpu.make_async_copy(taps_send2.at[my_ch], taps_recv2.at[my_ch], local_sem.at[2])
    own3.start()
    own3.wait()

    @pl.loop(1, CH)
    def _(k):
        p = ch_peer(k)
        ch_copy(taps_send2.at[p], taps_recv2.at[p], fs2.at[p], fr2.at[p], p).wait_recv()

    for sub in range(8):
        taps_wide[:, sub] = taps_recv2[:, :, pl.ds(TAPS * sub, TAPS)].astype(F32)

    row = lax.broadcasted_iota(jnp.int32, (TAPS, TAPS), 0)
    col = lax.broadcasted_iota(jnp.int32, (TAPS, TAPS), 1)
    keep = col >= row

    @pl.loop(0, MINE)
    def _(c):
        blocks[c, pl.ds(0, TAPS), :] = jnp.zeros((TAPS, TAPS), BF16)

        def build(j, prev):
            for sub in range(8):
                line = taps_wide[j, sub, pl.ds(c, 1), :]
                wide = jnp.broadcast_to(line, (TAPS, TAPS))
                rolled = pltpu.roll(wide, 0, 1, stride=1, stride_axis=0)
                start = pl.multiple_of((j * 8 + sub + 1) * TAPS, TAPS)
                blocks[c, pl.ds(start, TAPS), :] = jnp.where(keep, rolled, prev).astype(BF16)
                prev = rolled
            return prev

        lax.fori_loop(0, CH, build, jnp.zeros((TAPS, TAPS), F32))

    own2.wait()

    @pl.loop(1, CTX)
    def _(k):
        p = ctx_peer(k)
        ctx_copy(send.at[p], recv.at[p], ss.at[p], sr.at[p], p).wait_recv()

    for half in range(2):
        part = recv[:, :, :, pl.ds(TAPS * half, TAPS)].astype(F32)
        rows_in[half] = part.reshape(ROWS * 2 * MINE, TAPS)
    blank = jnp.zeros((ROWS, TAPS), F32)
    for half in range(2):
        shifted[0, half, pl.ds(0, ROWS), :] = blank
        shifted[1, half, pl.ds(ROWS, ROWS), :] = blank

    @pl.loop(0, MINE)
    def _(c):
        for half in range(2):
            shifted[0, half, pl.ds(ROWS, ROWS), :] = rows_in[half, pl.ds(c, ROWS, stride=2 * MINE), :]
            shifted[1, half, pl.ds(0, ROWS), :] = rows_in[half, pl.ds(c + MINE, ROWS, stride=2 * MINE), :]
        for s in range(SEGS):
            n = ROWS - PER * s
            for e in range(PER):
                far = PER * s + e
                for part in range(2):
                    half = 1 - part
                    lanes = pl.ds(e * BLK + part * TAPS, TAPS)
                    lhs[s, pl.ds(0, n), lanes] = shifted[0, half, pl.ds(ROWS - e, n), :].astype(BF16)
                    lhs[s, pl.ds(n, n), lanes] = shifted[1, half, pl.ds(far, n), :].astype(BF16)
        for s in range(SEGS):
            n = ROWS - PER * s
            depth = PER * BLK
            rhs = jnp.concatenate(
                [
                    blocks[c, pl.ds(depth * s, depth), :],
                    blocks[c, pl.ds(depth * s + TAPS, depth), :],
                ],
                axis=1,
            )
            out = jnp.dot(lhs[s, pl.ds(0, 2 * n), :], rhs, preferred_element_type=F32)
            if s == 0:
                acc[...] = out
            else:
                acc[pl.ds(PER * s, n), :] += out[:n]
                acc[pl.ds(ROWS, n), :] += out[n:]
        for half in range(2):
            lanes = pl.ds(TAPS * half, TAPS)
            rows_out[half, pl.ds(c, ROWS, stride=2 * MINE), :] = acc[pl.ds(0, ROWS), lanes]
            rows_out[half, pl.ds(c + MINE, ROWS, stride=2 * MINE), :] = acc[pl.ds(ROWS, ROWS), lanes]

    for half in range(2):
        part = rows_out[half].reshape(CTX, 2, 2 * MINE, TAPS)
        back_send[:, :, :, pl.ds(TAPS * half, TAPS)] = part.astype(BF16)

    @pl.loop(1, CTX)
    def _(k):
        p = ctx_peer(k)
        ctx_copy(back_send.at[p], back.at[me], bs.at[p], br.at[me], p).start()

    own4 = pltpu.make_async_copy(back_send.at[me], back.at[me], local_sem.at[3])
    own4.start()

    @pl.loop(1, CTX)
    def _(k):
        p = ctx_peer(k)
        ctx_copy(taps_send.at[p], taps_mid.at[p], fs1.at[p], fr1.at[p], p).wait_send()
        ctx_copy(send.at[p], recv.at[p], ss.at[p], sr.at[p], p).wait_send()

    @pl.loop(1, CH)
    def _(k):
        p = ch_peer(k)
        ch_copy(taps_send2.at[p], taps_recv2.at[p], fs2.at[p], fr2.at[p], p).wait_send()

    own4.wait()

    @pl.loop(1, CTX)
    def _(k):
        p = ctx_peer(k)
        done = ctx_copy(back_send.at[p], back.at[p], bs.at[p], br.at[p], p)
        done.wait_send()
        done.wait_recv()


def finish_kernel(query, key, value, grad, gain, back, output, query_grad, key_grad, value_grad):
    unit = eye(BLK)
    mirror = eye(BLK, True)
    scale = gain[...]
    for half in range(2):
        toks = pl.ds(BLK * half, BLK)
        wide = back[:, half].astype(F32)
        conv = wide[:, :MINE].reshape(CTX * MINE, BLK).astype(BF16)
        refl = wide[:, MINE:].reshape(CTX * MINE, BLK).astype(BF16)
        q = query[toks, :].astype(F32)
        k = key[toks, :].astype(F32)
        v = value[toks, :].astype(F32)
        g = grad[toks, :].astype(F32)
        summed = times_transposed(unit, conv) + scale * (k * v).astype(BF16).astype(F32)
        output[toks, :] = (q * summed).astype(BF16)
        query_grad[toks, :] = (g * summed).astype(BF16)
        grad_sum = times_transposed(mirror, refl) + scale * (g * q).astype(BF16).astype(F32)
        key_grad[toks, :] = (grad_sum * v).astype(BF16)
        value_grad[toks, :] = (grad_sum * k).astype(BF16)


def shards(query, key, value, grad, taps, gain):
    vmem = pl.BlockSpec(memory_space=pltpu.VMEM)
    dma = pltpu.SemaphoreType.DMA
    tile = (CTX, 2, 2 * MINE, BLK)
    back = pl.pallas_call(
        convolve_kernel,
        out_shape=jax.ShapeDtypeStruct(tile, BF16),
        in_specs=[vmem] * 5,
        out_specs=vmem,
        scratch_shapes=[
            pltpu.VMEM((CH * CTX, MINE, 32), F32),
            pltpu.VMEM((CTX, 32, CH * MINE), BF16),
            pltpu.VMEM((CTX, 32, CH * MINE), BF16),
            pltpu.VMEM((CH, MINE, 1024), BF16),
            pltpu.VMEM((CH, MINE, 1024), BF16),
            pltpu.VMEM((CH, 8, MINE, TAPS), F32),
            pltpu.VMEM(tile, BF16),
            pltpu.VMEM(tile, BF16),
            pltpu.VMEM((2, ROWS * 2 * MINE, TAPS), F32),
            pltpu.VMEM((2, ROWS * 2 * MINE, TAPS), F32),
            pltpu.VMEM(tile, BF16),
            pltpu.VMEM((MINE, (TBLK + 1) * TAPS, TAPS), BF16),
            pltpu.VMEM((2, 2, 2 * ROWS, TAPS), F32),
            pltpu.VMEM((SEGS, 2 * ROWS, PER * BLK), BF16),
            pltpu.VMEM((2 * ROWS, BLK), F32),
            dma((4,)),
            dma((CTX,)), dma((CTX,)),
            dma((CH,)), dma((CH,)),
            dma((CTX,)), dma((CTX,)),
            dma((CTX,)), dma((CTX,)),
        ],
        compiler_params=pltpu.CompilerParams(
            collective_id=0, has_side_effects=True, vmem_limit_bytes=60 * 2**20
        ),
        name="convolve",
    )(query, key, value, grad, taps)
    shape = jax.ShapeDtypeStruct(query.shape, BF16)
    return pl.pallas_call(
        finish_kernel,
        out_shape=(shape,) * 4,
        in_specs=[vmem] * 6,
        out_specs=(vmem,) * 4,
        name="finish",
    )(query, key, value, grad, gain.reshape(1, -1), back)


def solution(mesh):
    placed = (
        P("ctx", "ch"),
        P("ctx", "ch"),
        P("ctx", "ch"),
        P("ctx", "ch"),
        P(None, ("ch", "ctx")),
        P("ch"),
    )
    return jax.shard_map(
        shards,
        mesh=mesh,
        in_specs=placed,
        out_specs=(P("ctx", "ch"), P("ctx", "ch"), P("ctx", "ch"), P("ctx", "ch")),
        check_vma=False,
    )
```

profile of v0, /device:TPU:1, one launch (start us, length us, event | category | flops | bytes accessed | tf_op | source)
XLA Modules:
  0.0 101.9 jit_solution(4766757558750540211)
XLA Ops:
  0.6 2.3 %copy.10.taps = bf16[4096,32]{1,0:T(8,128)(2,1)} copy(bf16[4096,32]{0,1:T(8,128)(2,1)} %param.10) | data formatting | bytes 524288 | tf_op args[4]
  2.9 96.1 %convolve.1.back = bf16[32,2,16,256]{3,2,1,0:T(8,128)(2,1)} custom-call(bf16[512,256]{1,0:T(8,128)(2,1)} %query.3, bf16[512,256]{1,0:T(8,128)(2,1)} %key.3, bf16[512,256]{1,0:T(8,128)(2,1)} %value.3, bf16[512,256]{1,0:T(8,128)(2,1)} %grad.3, bf16[4096,32]{1,0:T(8,128)(2,1)} %copy.10.taps), custom_call_target="tpu_custom_call" | custom-call | tf_op jit(solution)/shard_map/convolve/pallas_call | solution.py:272
  99.0 2.9 %finish.1 = (bf16[512,256]{1,0:T(8,128)(2,1)}, bf16[512,256]{1,0:T(8,128)(2,1)}, bf16[512,256]{1,0:T(8,128)(2,1)}, bf16[512,256]{1,0:T(8,128)(2,1)}) custom-call(bf16[512,256]{1,0:T(8,128)(2,1)} %query.3, bf16[512,256]{1,0:T(8,128)(2,1)} %key.3, bf16[512,256]{1,0:T(8,128)(2,1)} %value.3, bf16[512,256]{1,0:T(8,128)(2,1)} %grad.3, f32[1,256]{1,0:T(1,128)} %bitcast.1, ...), custom_call_target="tpu_custom_call" | custom-call | tf_op jit(solution)/shard_map/finish/pallas_call | solution.py:305
where the time goes:
time: 102 us
  Pallas kernels  99 us (97%)
  local copies, waits for them, and re-layouts  2.29 us (2%)
    pallas_call x1, Pallas kernels, shards(): pl.pallas_call(convolve_kernel, out_shape=jax.ShapeDtypeStruct(tile, BF16...  96.1 us
    pallas_call x1, Pallas kernels, shards(): pl.pallas_call(finish_kernel, out_shape=(shape,) * 4, in_specs=[vmem] * 6...  2.86 us
    unnamed x1, local copies, waits for them, and re-layouts  2.29 us

commit v1 on v0

v1 whole, which is shorter than its diff:
```python
import jax
import jax.numpy as jnp
from jax import lax
from jax.experimental import pallas as pl
from jax.experimental.pallas import tpu as pltpu
from jax.sharding import PartitionSpec as P

CTX = 32
CH = 16
MINE = 8
ROWS = 64
BLK = 256
TAPS = 128
TBLK = 128
GROUPS = 4
STEP = 32
PAIR = MINE // GROUPS
SEGS = 4
PER = 16
MESH = pl.DeviceIdType.MESH
F32 = jnp.float32
BF16 = jnp.bfloat16


def eye(size, flip=False):
    row = lax.broadcasted_iota(jnp.int32, (size, size), 0)
    col = lax.broadcasted_iota(jnp.int32, (size, size), 1)
    if flip:
        col = size - 1 - col
    return (row == col).astype(F32).astype(BF16)


def spread(size):
    row = lax.broadcasted_iota(jnp.int32, (size, size), 0)
    col = lax.broadcasted_iota(jnp.int32, (size, size), 1)
    return (row == col % CTX * MINE + col // CTX).astype(F32).astype(BF16)


def times_transposed(left, right):
    return lax.dot_general(left, right, (((1,), (1,)), ((), ())), preferred_element_type=F32)


def gate(left, right):
    return (left.astype(F32) * right.astype(F32)).astype(BF16)


def remote(src, dst, send_sem, recv_sem, ctx, ch):
    return pltpu.make_async_remote_copy(
        src_ref=src, dst_ref=dst, send_sem=send_sem, recv_sem=recv_sem,
        device_id={"ctx": ctx, "ch": ch}, device_id_type=MESH,
    )


def convolve_kernel(
    query, key, value, grad, taps, back,
    taps_mid, taps_send, taps_recv, taps_wide,
    send, recv, rows_in, rows_out, back_send, blocks, shifted, lhs, acc,
    local_sem, fs1, fr1, fs2, fr2, ss, sr, bs, br,
):
    me = lax.axis_index("ctx")
    my_ch = lax.axis_index("ch")
    across = lax.rem(my_ch + CH // 2, CH)
    barrier = pltpu.get_barrier_semaphore()

    def ctx_peer(k):
        return lax.rem(me + k, CTX)

    def ch_peer(k):
        return lax.rem(my_ch + k, CH)

    @pl.loop(0, CTX)
    def _(k):
        where = {"ctx": ctx_peer(k), "ch": across}
        pl.semaphore_signal(barrier, inc=1, device_id=where, device_id_type=MESH)

    @pl.loop(1, CH)
    def _(k):
        where = {"ctx": me, "ch": ch_peer(k)}
        pl.semaphore_signal(barrier, inc=1, device_id=where, device_id_type=MESH)

    pl.semaphore_wait(barrier, CTX + CH - 1)

    def columns(p):
        return taps.at[:, pl.ds(pl.multiple_of(p * 256, 256), 256)]

    @pl.loop(1, CH)
    def _(k):
        p = ch_peer(k)
        remote(columns(p), taps_mid.at[my_ch], fs1.at[p], fr1.at[my_ch], me, p).start()

    own = pltpu.make_async_copy(columns(my_ch), taps_mid.at[my_ch], local_sem.at[0])
    own.start()

    order = spread(BLK)
    mirror = eye(BLK, True)
    for half in range(2):
        toks = pl.ds(BLK * half, BLK)
        gated = times_transposed(order, gate(key[toks, :], value[toks, :]))
        turned = jnp.dot(mirror, gate(grad[toks, :], query[toks, :]), preferred_element_type=F32)
        graded = times_transposed(order, turned.astype(BF16))
        both = jnp.concatenate(
            [gated.reshape(CTX, MINE, BLK), graded.reshape(CTX, MINE, BLK)], axis=1
        )
        send[:, half] = both.astype(BF16)

    own.wait()

    @pl.loop(1, CH)
    def _(k):
        p = ch_peer(k)
        remote(columns(p), taps_mid.at[p], fs1.at[p], fr1.at[p], me, p).wait_recv()

    for b in range(4):
        tile = taps_mid[pl.ds(4 * b, 4)].reshape(TAPS, 256)
        turned = times_transposed(order, tile)
        taps_send[:, :, pl.ds(TAPS * b, TAPS)] = turned.reshape(CTX, MINE, TAPS).astype(BF16)

    @pl.loop(0, CTX)
    def _(k):
        p = ctx_peer(k)
        remote(taps_send.at[p], taps_recv.at[me], fs2.at[p], fr2.at[me], p, across).start()

    @pl.loop(0, CTX)
    def _(k):
        p = ctx_peer(k)
        remote(send.at[p], recv.at[me], ss.at[p], sr.at[me], p, across).start()

    @pl.loop(0, CTX)
    def _(k):
        p = ctx_peer(k)
        remote(taps_send.at[p], taps_recv.at[p], fs2.at[p], fr2.at[p], p, across).wait_recv()

    lane = lax.broadcasted_iota(jnp.int32, (MINE, TAPS), 1)
    low_half = lane < 64
    low_quarter = lane % 64 < 32

    @pl.loop(0, 8)
    def _(m):
        for k in range(4):
            a, b, c, d = [
                taps_recv[4 * m + q, :, pl.ds(TAPS * k, TAPS)].astype(F32) for q in range(4)
            ]

            def swap(x, y, low, width):
                first = jnp.where(low, x, pltpu.roll(y, width, 1))
                second = jnp.where(low, pltpu.roll(x, TAPS - width, 1), y)
                return first, second

            a, c = swap(a, c, low_half, 64)
            b, d = swap(b, d, low_half, 64)
            a, b = swap(a, b, low_quarter, 32)
            c, d = swap(c, d, low_quarter, 32)
            for s, line in enumerate((a, b, c, d)):
                taps_wide[(4 * k + s) * 8 + m] = line

    row = lax.broadcasted_iota(jnp.int32, (TAPS, TAPS), 0)
    col = lax.broadcasted_iota(jnp.int32, (TAPS, TAPS), 1)
    keep = col >= row

    @pl.loop(0, MINE)
    def _(c):
        blocks[c, pl.ds(0, TAPS), :] = jnp.zeros((TAPS, TAPS), BF16)

        def build(j, prev):
            for sub in range(STEP):
                line = taps_wide[j * STEP + sub, pl.ds(c, 1), :]
                wide = jnp.broadcast_to(line, (TAPS, TAPS))
                rolled = pltpu.roll(wide, 0, 1, stride=1, stride_axis=0)
                start = pl.multiple_of((j * STEP + sub + 1) * TAPS, TAPS)
                blocks[c, pl.ds(start, TAPS), :] = jnp.where(keep, rolled, prev).astype(BF16)
                prev = rolled
            return prev

        lax.fori_loop(0, TBLK // STEP, build, jnp.zeros((TAPS, TAPS), F32))

    @pl.loop(0, CTX)
    def _(k):
        p = ctx_peer(k)
        remote(send.at[p], recv.at[p], ss.at[p], sr.at[p], p, across).wait_recv()

    for half in range(2):
        part = recv[:, :, :, pl.ds(TAPS * half, TAPS)].astype(F32)
        rows_in[half] = part.reshape(ROWS * 2 * MINE, TAPS)
    blank = jnp.zeros((ROWS, TAPS), F32)
    for half in range(2):
        shifted[0, half, pl.ds(0, ROWS), :] = blank
        shifted[1, half, pl.ds(ROWS, ROWS), :] = blank

    @pl.loop(0, GROUPS)
    def _(group):
        @pl.loop(0, PAIR)
        def _(r):
            c = group * PAIR + r
            for half in range(2):
                shifted[0, half, pl.ds(ROWS, ROWS), :] = rows_in[half, pl.ds(c, ROWS, stride=2 * MINE), :]
                shifted[1, half, pl.ds(0, ROWS), :] = rows_in[half, pl.ds(c + MINE, ROWS, stride=2 * MINE), :]
            for s in range(SEGS):
                n = ROWS - PER * s
                for e in range(PER):
                    far = PER * s + e
                    for part in range(2):
                        half = 1 - part
                        lanes = pl.ds(e * BLK + part * TAPS, TAPS)
                        lhs[s, pl.ds(0, n), lanes] = shifted[0, half, pl.ds(ROWS - e, n), :].astype(BF16)
                        lhs[s, pl.ds(n, n), lanes] = shifted[1, half, pl.ds(far, n), :].astype(BF16)
            for s in range(SEGS):
                n = ROWS - PER * s
                depth = PER * BLK
                rhs = jnp.concatenate(
                    [
                        blocks[c, pl.ds(depth * s, depth), :],
                        blocks[c, pl.ds(depth * s + TAPS, depth), :],
                    ],
                    axis=1,
                )
                out = jnp.dot(lhs[s, pl.ds(0, 2 * n), :], rhs, preferred_element_type=F32)
                if s == 0:
                    acc[...] = out
                else:
                    acc[pl.ds(PER * s, n), :] += out[:n]
                    acc[pl.ds(ROWS, n), :] += out[n:]
            for half in range(2):
                lanes = pl.ds(TAPS * half, TAPS)
                rows_out[half, pl.ds(r, ROWS, stride=2 * PAIR), :] = acc[pl.ds(0, ROWS), lanes]
                rows_out[half, pl.ds(r + PAIR, ROWS, stride=2 * PAIR), :] = acc[pl.ds(ROWS, ROWS), lanes]

        for half in range(2):
            part = rows_out[half].reshape(CTX, 4 * PAIR, TAPS)
            back_send[group, :, :, pl.ds(TAPS * half, TAPS)] = part.astype(BF16)

        @pl.loop(0, CTX)
        def _(k):
            p = ctx_peer(k)
            remote(
                back_send.at[group, p], back.at[group, me],
                bs.at[group, p], br.at[group, me], p, across,
            ).start()

    @pl.loop(1, CH)
    def _(k):
        p = ch_peer(k)
        remote(columns(p), taps_mid.at[p], fs1.at[p], fr1.at[p], me, p).wait_send()

    @pl.loop(0, CTX)
    def _(k):
        p = ctx_peer(k)
        remote(taps_send.at[p], taps_recv.at[p], fs2.at[p], fr2.at[p], p, across).wait_send()
        remote(send.at[p], recv.at[p], ss.at[p], sr.at[p], p, across).wait_send()

    @pl.loop(0, GROUPS)
    def _(group):
        @pl.loop(0, CTX)
        def _(k):
            p = ctx_peer(k)
            done = remote(
                back_send.at[group, p], back.at[group, p],
                bs.at[group, p], br.at[group, p], p, across,
            )
            done.wait_send()
            done.wait_recv()


def finish_kernel(query, key, value, grad, gain, back, output, query_grad, key_grad, value_grad, wide):
    unit = eye(BLK)
    mirror = eye(BLK, True)
    scale = gain[...]
    for part in range(2):
        lanes = pl.ds(TAPS * part, TAPS)
        wide[part] = back[:, :, :, lanes].astype(F32).reshape(GROUPS * CTX * 4 * PAIR, TAPS)

    def rows(first):
        columns = []
        for part in range(2):
            pieces = []
            for c in range(MINE):
                start = c // PAIR * (CTX * 4 * PAIR) + first + c % PAIR
                pieces.append(wide[part, pl.ds(start, CTX, stride=4 * PAIR), :])
            columns.append(jnp.concatenate(pieces, axis=0))
        return jnp.concatenate(columns, axis=1).astype(BF16)

    for half in range(2):
        toks = pl.ds(BLK * half, BLK)
        conv = rows(2 * PAIR * half)
        refl = rows(2 * PAIR * half + PAIR)
        q = query[toks, :].astype(F32)
        k = key[toks, :].astype(F32)
        v = value[toks, :].astype(F32)
        g = grad[toks, :].astype(F32)
        summed = times_transposed(unit, conv) + scale * (k * v).astype(BF16).astype(F32)
        output[toks, :] = (q * summed).astype(BF16)
        query_grad[toks, :] = (g * summed).astype(BF16)
        grad_sum = times_transposed(mirror, refl) + scale * (g * q).astype(BF16).astype(F32)
        key_grad[toks, :] = (grad_sum * v).astype(BF16)
        value_grad[toks, :] = (grad_sum * k).astype(BF16)


def shards(query, key, value, grad, taps, gain):
    vmem = pl.BlockSpec(memory_space=pltpu.VMEM)
    dma = pltpu.SemaphoreType.DMA
    tile = (CTX, 2, 2 * MINE, BLK)
    reply = (GROUPS, CTX, 4 * PAIR, BLK)
    back = pl.pallas_call(
        convolve_kernel,
        out_shape=jax.ShapeDtypeStruct(reply, BF16),
        in_specs=[vmem] * 5,
        out_specs=vmem,
        scratch_shapes=[
            pltpu.VMEM((CH, 32, 256), BF16),
            pltpu.VMEM((CTX, MINE, 512), BF16),
            pltpu.VMEM((CTX, MINE, 512), BF16),
            pltpu.VMEM((TBLK, MINE, TAPS), F32),
            pltpu.VMEM(tile, BF16),
            pltpu.VMEM(tile, BF16),
            pltpu.VMEM((2, ROWS * 2 * MINE, TAPS), F32),
            pltpu.VMEM((2, ROWS * 2 * PAIR, TAPS), F32),
            pltpu.VMEM(reply, BF16),
            pltpu.VMEM((MINE, (TBLK + 1) * TAPS, TAPS), BF16),
            pltpu.VMEM((2, 2, 2 * ROWS, TAPS), F32),
            pltpu.VMEM((SEGS, 2 * ROWS, PER * BLK), BF16),
            pltpu.VMEM((2 * ROWS, BLK), F32),
            dma((1,)),
            dma((CH,)), dma((CH,)),
            dma((CTX,)), dma((CTX,)),
            dma((CTX,)), dma((CTX,)),
            dma((GROUPS, CTX)), dma((GROUPS, CTX)),
        ],
        compiler_params=pltpu.CompilerParams(
            collective_id=0, has_side_effects=True, vmem_limit_bytes=60 * 2**20
        ),
        name="convolve",
    )(query, key, value, grad, taps.T)
    shape = jax.ShapeDtypeStruct(query.shape, BF16)
    return pl.pallas_call(
        finish_kernel,
        out_shape=(shape,) * 4,
        in_specs=[vmem] * 6,
        out_specs=(vmem,) * 4,
        scratch_shapes=[pltpu.VMEM((2, GROUPS * CTX * 4 * PAIR, TAPS), F32)],
        name="finish",
    )(query, key, value, grad, gain.reshape(1, -1), back)


def solution(mesh):
    placed = (
        P("ctx", "ch"),
        P("ctx", "ch"),
        P("ctx", "ch"),
        P("ctx", "ch"),
        P(None, ("ch", "ctx")),
        P("ch"),
    )
    return jax.shard_map(
        shards,
        mesh=mesh,
        in_specs=placed,
        out_specs=(P("ctx", "ch"), P("ctx", "ch"), P("ctx", "ch"), P("ctx", "ch")),
        check_vma=False,
    )
```

time: 102 us -> 79.4 us (0.78)
  Pallas kernels: 99 us -> 78.6 us
  local copies, waits for them, and re-layouts: 2.29 us -> 0 us
    pallas_call x1, Pallas kernels: 96.1 us -> 75.6 us  [shards(): pl.pallas_call(convolve_kernel, out_shape=jax.ShapeDtypeStruct(reply, BF1...]
    unnamed x1 -> x0, local copies, waits for them, and re-layouts: 2.29 us -> none
where the time goes in v1:
time: 79.4 us; the launch traced here: 79.2 us
  Pallas kernels  78.6 us (99%)
    pallas_call x1, Pallas kernels, shards(): pl.pallas_call(convolve_kernel, out_shape=jax.ShapeDtypeStruct(reply, BF1...  75.6 us
    pallas_call x1, Pallas kernels, shards(): pl.pallas_call(finish_kernel, out_shape=(shape,) * 4, in_specs=[vmem] * 6...  2.98 us

profile of v1, /device:TPU:1, one launch (start us, length us, event | category | flops | bytes accessed | tf_op | source)
XLA Modules:
  0.0 79.2 jit_solution(14901162521303014540)
XLA Ops:
  0.6 75.6 %convolve.1.back = bf16[4,32,8,256]{3,2,1,0:T(8,128)(2,1)} custom-call(bf16[512,256]{1,0:T(8,128)(2,1)} %query.3, bf16[512,256]{1,0:T(8,128)(2,1)} %key.3, bf16[512,256]{1,0:T(8,128)(2,1)} %value.3, bf16[512,256]{1,0:T(8,128)(2,1)} %grad.3, bf16[32,4096]{1,0:T(8,128)(2,1)} %bitcast.2), custom_call_target="tpu_custom_call" | custom-call | tf_op jit(solution)/shard_map/convolve/pallas_call | solution.py:302
  76.3 3.0 %finish.1 = (bf16[512,256]{1,0:T(8,128)(2,1)}, bf16[512,256]{1,0:T(8,128)(2,1)}, bf16[512,256]{1,0:T(8,128)(2,1)}, bf16[512,256]{1,0:T(8,128)(2,1)}) custom-call(bf16[512,256]{1,0:T(8,128)(2,1)} %query.3, bf16[512,256]{1,0:T(8,128)(2,1)} %key.3, bf16[512,256]{1,0:T(8,128)(2,1)} %value.3, bf16[512,256]{1,0:T(8,128)(2,1)} %grad.3, f32[1,256]{1,0:T(1,128)} %bitcast.3, ...), custom_call_target="tpu_custom_call" | custom-call | tf_op jit(solution)/shard_map/finish/pallas_call | solution.py:333

commit v2 on v1

--- a/solution.py
+++ b/solution.py
@@ -54,7 +54,7 @@
 def convolve_kernel(
     query, key, value, grad, taps, back,
     taps_mid, taps_send, taps_recv, taps_wide,
-    send, recv, rows_in, rows_out, back_send, blocks, shifted, lhs, acc,
+    send, recv, rows_in, rows_out, back_send, near, late, shifted, lhs, acc,
     local_sem, fs1, fr1, fs2, fr2, ss, sr, bs, br,
 ):
     me = lax.axis_index("ctx")
@@ -157,21 +157,25 @@
     col = lax.broadcasted_iota(jnp.int32, (TAPS, TAPS), 1)
     keep = col >= row
 
-    @pl.loop(0, MINE)
+    def build(blocks, slot, c, j, prev):
+        for sub in range(STEP):
+            line = taps_wide[j * STEP + sub, pl.ds(c, 1), :]
+            wide = jnp.broadcast_to(line, (TAPS, TAPS))
+            rolled = pltpu.roll(wide, 0, 1, stride=1, stride_axis=0)
+            start = (j * STEP + sub + 1) * TAPS
+            if not isinstance(j, int):
+                start = pl.multiple_of(start, TAPS)
+            blocks[slot, pl.ds(start, TAPS), :] = jnp.where(keep, rolled, prev).astype(BF16)
+            prev = rolled
+        return prev
+
+    @pl.loop(0, MINE // 2)
     def _(c):
-        blocks[c, pl.ds(0, TAPS), :] = jnp.zeros((TAPS, TAPS), BF16)
-
-        def build(j, prev):
-            for sub in range(STEP):
-                line = taps_wide[j * STEP + sub, pl.ds(c, 1), :]
-                wide = jnp.broadcast_to(line, (TAPS, TAPS))
-                rolled = pltpu.roll(wide, 0, 1, stride=1, stride_axis=0)
-                start = pl.multiple_of((j * STEP + sub + 1) * TAPS, TAPS)
-                blocks[c, pl.ds(start, TAPS), :] = jnp.where(keep, rolled, prev).astype(BF16)
-                prev = rolled
-            return prev
-
-        lax.fori_loop(0, TBLK // STEP, build, jnp.zeros((TAPS, TAPS), F32))
+        near[c, pl.ds(0, TAPS), :] = jnp.zeros((TAPS, TAPS), BF16)
+        late[c, pl.ds(0, TAPS), :] = jnp.zeros((TAPS, TAPS), BF16)
+        lax.fori_loop(
+            0, TBLK // STEP, lambda j, prev: build(near, c, c, j, prev), jnp.zeros((TAPS, TAPS), F32)
+        )
 
     @pl.loop(0, CTX)
     def _(k):
@@ -186,44 +190,44 @@
         shifted[0, half, pl.ds(0, ROWS), :] = blank
         shifted[1, half, pl.ds(ROWS, ROWS), :] = blank
 
-    @pl.loop(0, GROUPS)
-    def _(group):
-        @pl.loop(0, PAIR)
-        def _(r):
-            c = group * PAIR + r
-            for half in range(2):
-                shifted[0, half, pl.ds(ROWS, ROWS), :] = rows_in[half, pl.ds(c, ROWS, stride=2 * MINE), :]
-                shifted[1, half, pl.ds(0, ROWS), :] = rows_in[half, pl.ds(c + MINE, ROWS, stride=2 * MINE), :]
-            for s in range(SEGS):
-                n = ROWS - PER * s
-                for e in range(PER):
-                    far = PER * s + e
-                    for part in range(2):
-                        half = 1 - part
-                        lanes = pl.ds(e * BLK + part * TAPS, TAPS)
-                        lhs[s, pl.ds(0, n), lanes] = shifted[0, half, pl.ds(ROWS - e, n), :].astype(BF16)
-                        lhs[s, pl.ds(n, n), lanes] = shifted[1, half, pl.ds(far, n), :].astype(BF16)
-            for s in range(SEGS):
-                n = ROWS - PER * s
-                depth = PER * BLK
-                rhs = jnp.concatenate(
-                    [
-                        blocks[c, pl.ds(depth * s, depth), :],
-                        blocks[c, pl.ds(depth * s + TAPS, depth), :],
-                    ],
-                    axis=1,
-                )
-                out = jnp.dot(lhs[s, pl.ds(0, 2 * n), :], rhs, preferred_element_type=F32)
-                if s == 0:
-                    acc[...] = out
-                else:
-                    acc[pl.ds(PER * s, n), :] += out[:n]
-                    acc[pl.ds(ROWS, n), :] += out[n:]
-            for half in range(2):
-                lanes = pl.ds(TAPS * half, TAPS)
-                rows_out[half, pl.ds(r, ROWS, stride=2 * PAIR), :] = acc[pl.ds(0, ROWS), lanes]
-                rows_out[half, pl.ds(r + PAIR, ROWS, stride=2 * PAIR), :] = acc[pl.ds(ROWS, ROWS), lanes]
-
+    def channel(c, r, blocks, slot, ahead):
+        for half in range(2):
+            shifted[0, half, pl.ds(ROWS, ROWS), :] = rows_in[half, pl.ds(c, ROWS, stride=2 * MINE), :]
+            shifted[1, half, pl.ds(0, ROWS), :] = rows_in[half, pl.ds(c + MINE, ROWS, stride=2 * MINE), :]
+        for s in range(SEGS):
+            n = ROWS - PER * s
+            for e in range(PER):
+                far = PER * s + e
+                for part in range(2):
+                    half = 1 - part
+                    lanes = pl.ds(e * BLK + part * TAPS, TAPS)
+                    lhs[s, pl.ds(0, n), lanes] = shifted[0, half, pl.ds(ROWS - e, n), :].astype(BF16)
+                    lhs[s, pl.ds(n, n), lanes] = shifted[1, half, pl.ds(far, n), :].astype(BF16)
+        prev = jnp.zeros((TAPS, TAPS), F32)
+        for s in range(SEGS):
+            n = ROWS - PER * s
+            depth = PER * BLK
+            if ahead:
+                prev = build(late, slot, c + MINE // 2, s, prev)
+            rhs = jnp.concatenate(
+                [
+                    blocks[slot, pl.ds(depth * s, depth), :],
+                    blocks[slot, pl.ds(depth * s + TAPS, depth), :],
+                ],
+                axis=1,
+            )
+            out = jnp.dot(lhs[s, pl.ds(0, 2 * n), :], rhs, preferred_element_type=F32)
+            if s == 0:
+                acc[...] = out
+            else:
+                acc[pl.ds(PER * s, n), :] += out[:n]
+                acc[pl.ds(ROWS, n), :] += out[n:]
+        for half in range(2):
+            lanes = pl.ds(TAPS * half, TAPS)
+            rows_out[half, pl.ds(r, ROWS, stride=2 * PAIR), :] = acc[pl.ds(0, ROWS), lanes]
+            rows_out[half, pl.ds(r + PAIR, ROWS, stride=2 * PAIR), :] = acc[pl.ds(ROWS, ROWS), lanes]
+
+    def reply(group):
         for half in range(2):
             part = rows_out[half].reshape(CTX, 4 * PAIR, TAPS)
             back_send[group, :, :, pl.ds(TAPS * half, TAPS)] = part.astype(BF16)
@@ -235,6 +239,24 @@
                 back_send.at[group, p], back.at[group, me],
                 bs.at[group, p], br.at[group, me], p, across,
             ).start()
+
+    @pl.loop(0, GROUPS // 2)
+    def _(group):
+        @pl.loop(0, PAIR)
+        def _(r):
+            c = group * PAIR + r
+            channel(c, r, near, c, True)
+
+        reply(group)
+
+    @pl.loop(GROUPS // 2, GROUPS)
+    def _(group):
+        @pl.loop(0, PAIR)
+        def _(r):
+            c = group * PAIR + r
+            channel(c, r, late, c - MINE // 2, False)
+
+        reply(group)
 
     @pl.loop(1, CH)
     def _(k):
@@ -314,7 +336,8 @@
             pltpu.VMEM((2, ROWS * 2 * MINE, TAPS), F32),
             pltpu.VMEM((2, ROWS * 2 * PAIR, TAPS), F32),
             pltpu.VMEM(reply, BF16),
-            pltpu.VMEM((MINE, (TBLK + 1) * TAPS, TAPS), BF16),
+            pltpu.VMEM((MINE // 2, (TBLK + 1) * TAPS, TAPS), BF16),
+            pltpu.VMEM((MINE // 2, (TBLK + 1) * TAPS, TAPS), BF16),
             pltpu.VMEM((2, 2, 2 * ROWS, TAPS), F32),
             pltpu.VMEM((SEGS, 2 * ROWS, PER * BLK), BF16),
             pltpu.VMEM((2 * ROWS, BLK), F32),

time: 79.4 us -> 75.7 us (0.953)
  Pallas kernels: 78.6 us -> 74.9 us
    pallas_call x1, Pallas kernels: 75.6 us -> 71.9 us  [shards(): pl.pallas_call(convolve_kernel, out_shape=jax.ShapeDtypeStruct(reply, BF1...]
where the time goes in v2:
time: 75.7 us; the launch traced here: 75.6 us
  Pallas kernels  74.9 us (99%)
    pallas_call x1, Pallas kernels, shards(): pl.pallas_call(convolve_kernel, out_shape=jax.ShapeDtypeStruct(reply, BF1...  71.9 us
    pallas_call x1, Pallas kernels, shards(): pl.pallas_call(finish_kernel, out_shape=(shape,) * 4, in_specs=[vmem] * 6...  2.97 us

profile of v2, /device:TPU:1, one launch (start us, length us, event | category | flops | bytes accessed | tf_op | source)
XLA Modules:
  0.0 75.6 jit_solution(10029757953079532069)
XLA Ops:
  0.6 71.9 %convolve.1.back = bf16[4,32,8,256]{3,2,1,0:T(8,128)(2,1)} custom-call(bf16[512,256]{1,0:T(8,128)(2,1)} %query.3, bf16[512,256]{1,0:T(8,128)(2,1)} %key.3, bf16[512,256]{1,0:T(8,128)(2,1)} %value.3, bf16[512,256]{1,0:T(8,128)(2,1)} %grad.3, bf16[32,4096]{1,0:T(8,128)(2,1)} %bitcast.2), custom_call_target="tpu_custom_call" | custom-call | tf_op jit(solution)/shard_map/convolve/pallas_call | solution.py:324
  72.6 3.0 %finish.1 = (bf16[512,256]{1,0:T(8,128)(2,1)}, bf16[512,256]{1,0:T(8,128)(2,1)}, bf16[512,256]{1,0:T(8,128)(2,1)}, bf16[512,256]{1,0:T(8,128)(2,1)}) custom-call(bf16[512,256]{1,0:T(8,128)(2,1)} %query.3, bf16[512,256]{1,0:T(8,128)(2,1)} %key.3, bf16[512,256]{1,0:T(8,128)(2,1)} %value.3, bf16[512,256]{1,0:T(8,128)(2,1)} %grad.3, f32[1,256]{1,0:T(1,128)} %bitcast.3, ...), custom_call_target="tpu_custom_call" | custom-call | tf_op jit(solution)/shard_map/finish/pallas_call | solution.py:356

commit v3 on v2

--- a/solution.py
+++ b/solution.py
@@ -52,10 +52,10 @@
 
 
 def convolve_kernel(
-    query, key, value, grad, taps, back,
-    taps_mid, taps_send, taps_recv, taps_wide,
+    query_in, key_in, value_in, grad_in, taps_in, back,
+    query, key, value, grad, taps, taps_mid, taps_send, taps_recv, taps_wide,
     send, recv, rows_in, rows_out, back_send, near, late, shifted, lhs, acc,
-    local_sem, fs1, fr1, fs2, fr2, ss, sr, bs, br,
+    local_sem, in_sem, fs1, fr1, fs2, fr2, ss, sr, bs, br,
 ):
     me = lax.axis_index("ctx")
     my_ch = lax.axis_index("ch")
@@ -78,6 +78,15 @@
         where = {"ctx": me, "ch": ch_peer(k)}
         pl.semaphore_signal(barrier, inc=1, device_id=where, device_id_type=MESH)
 
+    loads = [
+        pltpu.make_async_copy(src, dst, in_sem.at[index])
+        for index, (src, dst) in enumerate(
+            ((taps_in, taps), (key_in, key), (value_in, value), (grad_in, grad), (query_in, query))
+        )
+    ]
+    for load in loads:
+        load.start()
+    loads[0].wait()
     pl.semaphore_wait(barrier, CTX + CH - 1)
 
     def columns(p):
@@ -91,6 +100,8 @@
     own = pltpu.make_async_copy(columns(my_ch), taps_mid.at[my_ch], local_sem.at[0])
     own.start()
 
+    for load in loads[1:]:
+        load.wait()
     order = spread(BLK)
     mirror = eye(BLK, True)
     for half in range(2):
@@ -318,15 +329,21 @@
 
 def shards(query, key, value, grad, taps, gain):
     vmem = pl.BlockSpec(memory_space=pltpu.VMEM)
+    anywhere = pl.BlockSpec(memory_space=pl.ANY)
     dma = pltpu.SemaphoreType.DMA
     tile = (CTX, 2, 2 * MINE, BLK)
     reply = (GROUPS, CTX, 4 * PAIR, BLK)
     back = pl.pallas_call(
         convolve_kernel,
         out_shape=jax.ShapeDtypeStruct(reply, BF16),
-        in_specs=[vmem] * 5,
-        out_specs=vmem,
+        in_specs=[anywhere] * 5,
+        out_specs=anywhere,
         scratch_shapes=[
+            pltpu.VMEM(query.shape, BF16),
+            pltpu.VMEM(query.shape, BF16),
+            pltpu.VMEM(query.shape, BF16),
+            pltpu.VMEM(query.shape, BF16),
+            pltpu.VMEM((32, CH * 256), BF16),
             pltpu.VMEM((CH, 32, 256), BF16),
             pltpu.VMEM((CTX, MINE, 512), BF16),
             pltpu.VMEM((CTX, MINE, 512), BF16),
@@ -341,7 +358,7 @@
             pltpu.VMEM((2, 2, 2 * ROWS, TAPS), F32),
             pltpu.VMEM((SEGS, 2 * ROWS, PER * BLK), BF16),
             pltpu.VMEM((2 * ROWS, BLK), F32),
-            dma((1,)),
+            dma((1,)), dma((5,)),
             dma((CH,)), dma((CH,)),
             dma((CTX,)), dma((CTX,)),
             dma((CTX,)), dma((CTX,)),

time: 75.7 us -> 74.5 us (0.984)
  Pallas kernels: 74.9 us -> 73.7 us
    pallas_call x1, Pallas kernels: 71.9 us -> 70.7 us  [shards(): pl.pallas_call(convolve_kernel, out_shape=jax.ShapeDtypeStruct(reply, BF1...]
where the time goes in v3:
time: 74.5 us; the launch traced here: 74.3 us
  Pallas kernels  73.7 us (99%)
    pallas_call x1, Pallas kernels, shards(): pl.pallas_call(convolve_kernel, out_shape=jax.ShapeDtypeStruct(reply, BF1...  70.7 us
    pallas_call x1, Pallas kernels, shards(): pl.pallas_call(finish_kernel, out_shape=(shape,) * 4, in_specs=[vmem] * 6...  2.98 us

profile of v3, /device:TPU:1, one launch (start us, length us, event | category | flops | bytes accessed | tf_op | source)
XLA Modules:
  0.0 74.3 jit_solution(4650891164619592568)
XLA Ops:
  0.6 70.7 %convolve.1.back = bf16[4,32,8,256]{3,2,1,0:T(8,128)(2,1)} custom-call(bf16[512,256]{1,0:T(8,128)(2,1)} %query.1, bf16[512,256]{1,0:T(8,128)(2,1)} %key.1, bf16[512,256]{1,0:T(8,128)(2,1)} %value.1, bf16[512,256]{1,0:T(8,128)(2,1)} %grad.1, bf16[32,4096]{1,0:T(8,128)(2,1)} %bitcast.2), custom_call_target="tpu_custom_call" | custom-call | tf_op jit(solution)/shard_map/convolve/pallas_call | solution.py:336
  71.4 3.0 %finish.1 = (bf16[512,256]{1,0:T(8,128)(2,1)}, bf16[512,256]{1,0:T(8,128)(2,1)}, bf16[512,256]{1,0:T(8,128)(2,1)}, bf16[512,256]{1,0:T(8,128)(2,1)}) custom-call(bf16[512,256]{1,0:T(8,128)(2,1)} %query.1, bf16[512,256]{1,0:T(8,128)(2,1)} %key.1, bf16[512,256]{1,0:T(8,128)(2,1)} %value.1, bf16[512,256]{1,0:T(8,128)(2,1)} %grad.1, f32[1,256]{1,0:T(1,128)} %bitcast.3, ...), custom_call_target="tpu_custom_call" | custom-call | tf_op jit(solution)/shard_map/finish/pallas_call | solution.py:373

commit v4 on v3

--- a/solution.py
+++ b/solution.py
@@ -90,7 +90,10 @@
     pl.semaphore_wait(barrier, CTX + CH - 1)
 
     def columns(p):
-        return taps.at[:, pl.ds(pl.multiple_of(p * 256, 256), 256)]
+        start = p * 256
+        if not isinstance(p, int):
+            start = pl.multiple_of(start, 256)
+        return taps.at[:, pl.ds(start, 256)]
 
     @pl.loop(1, CH)
     def _(k):
@@ -116,12 +119,13 @@
 
     own.wait()
 
-    @pl.loop(1, CH)
-    def _(k):
-        p = ch_peer(k)
-        remote(columns(p), taps_mid.at[p], fs1.at[p], fr1.at[p], me, p).wait_recv()
-
     for b in range(4):
+        for p in range(4 * b, 4 * b + 4):
+
+            @pl.when(my_ch != p)
+            def _(p=p):
+                remote(columns(p), taps_mid.at[p], fs1.at[p], fr1.at[p], me, p).wait_recv()
+
         tile = taps_mid[pl.ds(4 * b, 4)].reshape(TAPS, 256)
         turned = times_transposed(order, tile)
         taps_send[:, :, pl.ds(TAPS * b, TAPS)] = turned.reshape(CTX, MINE, TAPS).astype(BF16)
@@ -136,17 +140,15 @@
         p = ctx_peer(k)
         remote(send.at[p], recv.at[me], ss.at[p], sr.at[me], p, across).start()
 
-    @pl.loop(0, CTX)
-    def _(k):
-        p = ctx_peer(k)
-        remote(taps_send.at[p], taps_recv.at[p], fs2.at[p], fr2.at[p], p, across).wait_recv()
-
     lane = lax.broadcasted_iota(jnp.int32, (MINE, TAPS), 1)
     low_half = lane < 64
     low_quarter = lane % 64 < 32
 
     @pl.loop(0, 8)
     def _(m):
+        for q in range(4):
+            p = 4 * m + q
+            remote(taps_send.at[p], taps_recv.at[p], fs2.at[p], fr2.at[p], p, across).wait_recv()
         for k in range(4):
             a, b, c, d = [
                 taps_recv[4 * m + q, :, pl.ds(TAPS * k, TAPS)].astype(F32) for q in range(4)
@@ -188,18 +190,18 @@
             0, TBLK // STEP, lambda j, prev: build(near, c, c, j, prev), jnp.zeros((TAPS, TAPS), F32)
         )
 
-    @pl.loop(0, CTX)
-    def _(k):
-        p = ctx_peer(k)
-        remote(send.at[p], recv.at[p], ss.at[p], sr.at[p], p, across).wait_recv()
-
-    for half in range(2):
-        part = recv[:, :, :, pl.ds(TAPS * half, TAPS)].astype(F32)
-        rows_in[half] = part.reshape(ROWS * 2 * MINE, TAPS)
     blank = jnp.zeros((ROWS, TAPS), F32)
     for half in range(2):
         shifted[0, half, pl.ds(0, ROWS), :] = blank
         shifted[1, half, pl.ds(ROWS, ROWS), :] = blank
+
+    @pl.loop(0, CTX)
+    def _(p):
+        remote(send.at[p], recv.at[p], ss.at[p], sr.at[p], p, across).wait_recv()
+        for half in range(2):
+            part = recv[p, :, :, pl.ds(TAPS * half, TAPS)].astype(F32)
+            start = pl.multiple_of(p * 4 * MINE, 4 * MINE)
+            rows_in[half, pl.ds(start, 4 * MINE), :] = part.reshape(4 * MINE, TAPS)
 
     def channel(c, r, blocks, slot, ahead):
         for half in range(2):

time: 74.5 us -> 74.7 us (level)
  no operation moved by 1% of the time
where the time goes in v4:
time: 74.7 us; the launch traced here: 74.5 us
  Pallas kernels  73.9 us (99%)
    pallas_call x1, Pallas kernels, shards(): pl.pallas_call(convolve_kernel, out_shape=jax.ShapeDtypeStruct(reply, BF1...  70.9 us
    pallas_call x1, Pallas kernels, shards(): pl.pallas_call(finish_kernel, out_shape=(shape,) * 4, in_specs=[vmem] * 6...  2.98 us

profile of v4, /device:TPU:1, one launch (start us, length us, event | category | flops | bytes accessed | tf_op | source)
XLA Modules:
  0.0 74.5 jit_solution(3250328812415612230)
XLA Ops:
  0.6 70.9 %convolve.1.back = bf16[4,32,8,256]{3,2,1,0:T(8,128)(2,1)} custom-call(bf16[512,256]{1,0:T(8,128)(2,1)} %query.1, bf16[512,256]{1,0:T(8,128)(2,1)} %key.1, bf16[512,256]{1,0:T(8,128)(2,1)} %value.1, bf16[512,256]{1,0:T(8,128)(2,1)} %grad.1, bf16[32,4096]{1,0:T(8,128)(2,1)} %bitcast.2), custom_call_target="tpu_custom_call" | custom-call | tf_op jit(solution)/shard_map/convolve/pallas_call | solution.py:338
  71.5 3.0 %finish.1 = (bf16[512,256]{1,0:T(8,128)(2,1)}, bf16[512,256]{1,0:T(8,128)(2,1)}, bf16[512,256]{1,0:T(8,128)(2,1)}, bf16[512,256]{1,0:T(8,128)(2,1)}) custom-call(bf16[512,256]{1,0:T(8,128)(2,1)} %query.1, bf16[512,256]{1,0:T(8,128)(2,1)} %key.1, bf16[512,256]{1,0:T(8,128)(2,1)} %value.1, bf16[512,256]{1,0:T(8,128)(2,1)} %grad.1, f32[1,256]{1,0:T(1,128)} %bitcast.3, ...), custom_call_target="tpu_custom_call" | custom-call | tf_op jit(solution)/shard_map/finish/pallas_call | solution.py:375
